TPU v7x, 32 devices: a whole 2x2x4 slice. The times are simulated.
32 devices in a mesh: dp: 4 (over y, x), seg: 8 (over z, core).
Axes of the slice: x: 2, y: 2, z: 4, core: 2. Of those that a mesh axis runs over, the one named last changes fastest.
Arguments:
- inputs: bfloat16 [4, 4096, 768], P('dp', 'seg'), may hold values from -6 to 6
- doc_ids: int32 [4, 32], P('dp'), may hold values from 0 to 7, never falling along the last dimension, each value on 1 to 16 neighbouring positions
- cotangent: bfloat16 [4, 4096, 768], P('dp', 'seg'), may hold values from -6 to 6
- query_weight: bfloat16 [2, 768, 768], P(None, 'dp'), may hold values from -0.21875 to 0.21875
- query_bias: bfloat16 [2, 768], replicated, may hold values from -3 to 3
- key_weight: bfloat16 [2, 768, 768], P(None, 'dp'), may hold values from -0.21875 to 0.21875
- value_weight: bfloat16 [2, 768, 768], P(None, 'dp'), may hold values from -0.21875 to 0.21875
- value_bias: bfloat16 [2, 768], replicated, may hold values from -3 to 3
- out_weight: bfloat16 [2, 768, 768], P(None, 'dp'), may hold values from -1.75 to 1.75
- out_bias: bfloat16 [2, 768], replicated, may hold values from -3 to 3
- first_gain: bfloat16 [2, 768], replicated, may hold values from 0.5 to 1.5
- first_shift: bfloat16 [2, 768], replicated, may hold values from -2 to 2
- inner_weight: bfloat16 [2, 768, 3072], P(None, 'dp'), may hold values from -0.21875 to 0.21875
- inner_bias: bfloat16 [2, 3072], replicated, may hold values from -3 to 3
- outer_weight: bfloat16 [2, 3072, 768], P(None, 'dp'), may hold values from -0.109375 to 0.109375
- outer_bias: bfloat16 [2, 768], replicated, may hold values from -3 to 3
- second_gain: bfloat16 [2, 768], replicated, may hold values from 0.5 to 1.5
- second_shift: bfloat16 [2, 768], replicated, may hold values from -2 to 2
- segment_embed: bfloat16 [32, 768], replicated, may hold values from -3 to 3
Outputs:
- output: bfloat16 [4, 4096, 768], P('dp', 'seg')
- input_grad: bfloat16 [4, 4096, 768], P('dp', 'seg')
- grad_query_weight: float32 [2, 768, 768], P(None, 'dp')
- grad_query_bias: float32 [2, 768], P(None, 'dp')
- grad_key_weight: float32 [2, 768, 768], P(None, 'dp')
- grad_value_weight: float32 [2, 768, 768], P(None, 'dp')
- grad_value_bias: float32 [2, 768], P(None, 'dp')
- grad_out_weight: float32 [2, 768, 768], P(None, 'dp')
- grad_out_bias: float32 [2, 768], P(None, 'dp')
- grad_first_gain: float32 [2, 768], P(None, 'dp')
- grad_first_shift: float32 [2, 768], P(None, 'dp')
- grad_inner_weight: float32 [2, 768, 3072], P(None, 'dp')
- grad_inner_bias: float32 [2, 3072], P(None, 'dp')
- grad_outer_weight: float32 [2, 3072, 768], P(None, 'dp')
- grad_outer_bias: float32 [2, 768], P(None, 'dp')
- grad_second_gain: float32 [2, 768], P(None, 'dp')
- grad_second_shift: float32 [2, 768], P(None, 'dp')
- grad_segment_embed: float32 [32, 768], P(None, 'dp')
Inputs may be any that keep to these rules, and one draw needn't show every extreme that they name: `doc_ids`: along each row document numbers never fall; each document covers one to half of 32 consecutive segments, and some document of each row covers exactly half of 32.
All inputs are finite; a program needn't handle non-finite values.
Results may differ from a plain program's by a relative error of at most 0.02.
Values may be sent and summed in bfloat16 or wider, within the bound.
A program may use at most 256 MiB of HBM per device.

v0:
```python
import jax
import jax.numpy as jnp
from jax import lax
from jax.sharding import PartitionSpec as P

HEADS = 12
HEAD_DIM = 64
SEG_LEN = 128
epsilon = 1e-05


def normalize(values, gain, shift):
    centred = values - jnp.mean(values, axis=-1, keepdims=True)
    spread = jnp.mean(centred * centred, axis=-1, keepdims=True)
    return centred * lax.rsqrt(spread + epsilon) * gain + shift


def gelu_exact(values):
    return jax.nn.gelu(values, approximate=False)


def project(values, weight):
    return jnp.einsum("gnd,de->gne", values, weight, preferred_element_type=jnp.float32)


def back_project(values, weight):
    return jnp.einsum("gne,de->gnd", values, weight, preferred_element_type=jnp.float32)


def weight_grad(source, grads):
    return jnp.einsum("gnd,gne->de", source, grads, preferred_element_type=jnp.float32)


def row_total(values):
    return jnp.sum(values.astype(jnp.float32), axis=(0, 1))


def keep_pair(first_part, second_part):
    return (first_part, second_part)


def forward_layer(params, source, allowed, spread_keys):
    (
        query_weight,
        query_bias,
        key_weight,
        value_weight,
        value_bias,
        out_weight,
        out_bias,
        first_gain,
        first_shift,
        inner_weight,
        inner_bias,
        outer_weight,
        outer_bias,
        second_gain,
        second_shift,
    ) = params
    groups, length, width = source.shape
    queries = (project(source, query_weight) + query_bias.astype(jnp.float32)).astype(jnp.bfloat16)
    key_rows = project(source, key_weight).astype(jnp.bfloat16)
    value_rows = (project(source, value_weight) + value_bias.astype(jnp.float32)).astype(
        jnp.bfloat16
    )
    key_all, value_all = spread_keys(key_rows, value_rows)
    key_length = key_all.shape[1]
    query_heads = queries.reshape(groups, length, HEADS, HEAD_DIM)
    key_heads = key_all.reshape(groups, key_length, HEADS, HEAD_DIM)
    value_heads = value_all.reshape(groups, key_length, HEADS, HEAD_DIM)
    scores = (
        jnp.einsum("gqhe,gkhe->ghqk", query_heads, key_heads, preferred_element_type=jnp.float32)
        * 0.125
    )
    if allowed is not None:
        scores = jnp.where(allowed[:, None], scores, -1e30)
    attend = jax.nn.softmax(scores, axis=-1)
    attend_low = attend.astype(jnp.bfloat16)
    mixed = jnp.einsum(
        "ghqk,gkhe->gqhe", attend_low, value_heads, preferred_element_type=jnp.float32
    )
    mixed = mixed.astype(jnp.bfloat16).reshape(groups, length, width)
    branch = project(mixed, out_weight) + out_bias.astype(jnp.float32)
    hidden, first_pull = jax.vjp(
        normalize,
        source.astype(jnp.float32) + branch,
        first_gain.astype(jnp.float32),
        first_shift.astype(jnp.float32),
    )
    hidden_low = hidden.astype(jnp.bfloat16)
    inner = project(hidden_low, inner_weight) + inner_bias.astype(jnp.float32)
    active, gelu_pull = jax.vjp(gelu_exact, inner)
    active_low = active.astype(jnp.bfloat16)
    outer = project(active_low, outer_weight) + outer_bias.astype(jnp.float32)
    result, second_pull = jax.vjp(
        normalize, hidden + outer, second_gain.astype(jnp.float32), second_shift.astype(jnp.float32)
    )
    stored = (
        source,
        query_heads,
        key_heads,
        value_heads,
        attend,
        attend_low,
        mixed,
        first_pull,
        hidden_low,
        gelu_pull,
        active_low,
        second_pull,
    )
    return (result, stored)


def backward_layer(params, stored, grad_result, collect_keys):
    (
        query_weight,
        query_bias,
        key_weight,
        value_weight,
        value_bias,
        out_weight,
        out_bias,
        first_gain,
        first_shift,
        inner_weight,
        inner_bias,
        outer_weight,
        outer_bias,
        second_gain,
        second_shift,
    ) = params
    (
        source,
        query_heads,
        key_heads,
        value_heads,
        attend,
        attend_low,
        mixed,
        first_pull,
        hidden_low,
        gelu_pull,
        active_low,
        second_pull,
    ) = stored
    groups, length, width = source.shape
    key_length = key_heads.shape[1]
    grad_second_sum, grad_second_gain, grad_second_shift = second_pull(grad_result)
    grad_outer = grad_second_sum.astype(jnp.bfloat16)
    grad_outer_bias = row_total(grad_outer)
    grad_outer_weight = weight_grad(active_low, grad_outer)
    grad_active = back_project(grad_outer, outer_weight).astype(jnp.bfloat16)
    (grad_inner,) = gelu_pull(grad_active.astype(jnp.float32))
    grad_inner_low = grad_inner.astype(jnp.bfloat16)
    grad_inner_bias = row_total(grad_inner_low)
    grad_inner_weight = weight_grad(hidden_low, grad_inner_low)
    grad_hidden = grad_second_sum + back_project(grad_inner_low, inner_weight)
    grad_first_sum, grad_first_gain, grad_first_shift = first_pull(grad_hidden)
    grad_branch = grad_first_sum.astype(jnp.bfloat16)
    grad_out_bias = row_total(grad_branch)
    grad_out_weight = weight_grad(mixed, grad_branch)
    grad_mixed = back_project(grad_branch, out_weight).astype(jnp.bfloat16)
    grad_mixed = grad_mixed.reshape(groups, length, HEADS, HEAD_DIM)
    grad_attend = jnp.einsum(
        "gqhe,gkhe->ghqk", grad_mixed, value_heads, preferred_element_type=jnp.float32
    )
    grad_attend = grad_attend.astype(jnp.bfloat16).astype(jnp.float32)
    grad_value = jnp.einsum(
        "ghqk,gqhe->gkhe", attend_low, grad_mixed, preferred_element_type=jnp.float32
    )
    grad_value = grad_value.reshape(groups, key_length, width)
    grad_scores = attend * (grad_attend - jnp.sum(attend * grad_attend, axis=-1, keepdims=True))
    grad_scores = grad_scores.astype(jnp.bfloat16)
    grad_query = (
        jnp.einsum("ghqk,gkhe->gqhe", grad_scores, key_heads, preferred_element_type=jnp.float32)
        * 0.125
    )
    grad_query = grad_query.astype(jnp.bfloat16).reshape(groups, length, width)
    grad_key = (
        jnp.einsum("ghqk,gqhe->gkhe", grad_scores, query_heads, preferred_element_type=jnp.float32)
        * 0.125
    )
    grad_key = grad_key.reshape(groups, key_length, width)
    grad_key, grad_value = collect_keys(grad_key, grad_value)
    grad_key = grad_key.astype(jnp.bfloat16)
    grad_value = grad_value.astype(jnp.bfloat16)
    grad_source = (
        grad_first_sum
        + back_project(grad_query, query_weight)
        + back_project(grad_key, key_weight)
        + back_project(grad_value, value_weight)
    )
    gradients = (
        weight_grad(source, grad_query),
        row_total(grad_query),
        weight_grad(source, grad_key),
        weight_grad(source, grad_value),
        row_total(grad_value),
        grad_out_weight,
        grad_out_bias,
        grad_first_gain,
        grad_first_shift,
        grad_inner_weight,
        grad_inner_bias,
        grad_outer_weight,
        grad_outer_bias,
        grad_second_gain,
        grad_second_shift,
    )
    return (grad_source, gradients)


def shards(
    inputs,
    doc_ids,
    cotangent,
    query_weight,
    query_bias,
    key_weight,
    value_weight,
    value_bias,
    out_weight,
    out_bias,
    first_gain,
    first_shift,
    inner_weight,
    inner_bias,
    outer_weight,
    outer_bias,
    second_gain,
    second_shift,
    segment_embed,
):
    seg_count = lax.axis_size("seg")
    seg_index = lax.axis_index("seg")
    group_rows, local_length, width = inputs.shape
    seg_local = local_length // SEG_LEN
    query_full, key_full, value_full, out_full, inner_full, outer_full = (
        lax.all_gather(query_weight, "dp", axis=1, tiled=True),
        lax.all_gather(key_weight, "dp", axis=1, tiled=True),
        lax.all_gather(value_weight, "dp", axis=1, tiled=True),
        lax.all_gather(out_weight, "dp", axis=1, tiled=True),
        lax.all_gather(inner_weight, "dp", axis=1, tiled=True),
        lax.all_gather(outer_weight, "dp", axis=1, tiled=True),
    )
    stacked = (
        query_full,
        query_bias,
        key_full,
        value_full,
        value_bias,
        out_full,
        out_bias,
        first_gain,
        first_shift,
        inner_full,
        inner_bias,
        outer_full,
        outer_bias,
        second_gain,
        second_shift,
    )
    first_params = tuple((weight[0] for weight in stacked))
    cross_params = tuple((weight[1] for weight in stacked))
    pieces = inputs.reshape(group_rows * seg_local, SEG_LEN, width)
    segment_out, segment_stored = forward_layer(first_params, pieces, None, keep_pair)
    segment_grid = segment_out.reshape(group_rows, seg_local, SEG_LEN, width)
    position = lax.dynamic_slice_in_dim(segment_embed, seg_index * seg_local, seg_local, 0).astype(
        jnp.float32
    )
    heads_in = (segment_grid[:, :, 0, :] + position).astype(jnp.bfloat16)
    row_input = lax.all_gather(heads_in, "seg", axis=1, tiled=True)
    allowed = doc_ids[:, :, None] == doc_ids[:, None, :]
    cross_out, cross_stored = forward_layer(cross_params, row_input, allowed, keep_pair)
    returned = lax.dynamic_slice_in_dim(cross_out, seg_index * seg_local, seg_local, 1).astype(
        jnp.bfloat16
    )
    output = jnp.concatenate(
        [returned[:, :, None, :], segment_grid[:, :, 1:, :].astype(jnp.bfloat16)], axis=2
    )
    output = output.reshape(group_rows, local_length, width)
    cot_grid = cotangent.reshape(group_rows, seg_local, SEG_LEN, width)
    cot_heads = cot_grid[:, :, 0, :]
    grad_cross = lax.all_gather(cot_heads, "seg", axis=1, tiled=True)
    grad_row_input, cross_grads = backward_layer(
        cross_params, cross_stored, grad_cross.astype(jnp.float32), keep_pair
    )
    grad_row_low = grad_row_input.astype(jnp.bfloat16)
    factor = 1.0 / seg_count
    embed_grad = jnp.sum(grad_row_low.astype(jnp.float32), axis=0) * factor
    cross_grads = tuple((part * factor for part in cross_grads))
    grad_heads = lax.dynamic_slice_in_dim(grad_row_low, seg_index * seg_local, seg_local, 1)
    grad_grid = jnp.concatenate(
        [grad_heads[:, :, None, :].astype(jnp.float32), cot_grid[:, :, 1:, :].astype(jnp.float32)],
        axis=2,
    )
    grad_grid = grad_grid.reshape(group_rows * seg_local, SEG_LEN, width)
    grad_pieces, segment_grads = backward_layer(first_params, segment_stored, grad_grid, keep_pair)
    input_grad = grad_pieces.astype(jnp.bfloat16).reshape(group_rows, local_length, width)
    shares = (
        lax.psum_scatter(segment_grads[0], "dp", scatter_dimension=0, tiled=True),
        lax.psum_scatter(segment_grads[1], "dp", scatter_dimension=0, tiled=True),
        lax.psum_scatter(segment_grads[2], "dp", scatter_dimension=0, tiled=True),
        lax.psum_scatter(segment_grads[3], "dp", scatter_dimension=0, tiled=True),
        lax.psum_scatter(segment_grads[4], "dp", scatter_dimension=0, tiled=True),
        lax.psum_scatter(segment_grads[5], "dp", scatter_dimension=0, tiled=True),
        lax.psum_scatter(segment_grads[6], "dp", scatter_dimension=0, tiled=True),
        lax.psum_scatter(segment_grads[7], "dp", scatter_dimension=0, tiled=True),
        lax.psum_scatter(segment_grads[8], "dp", scatter_dimension=0, tiled=True),
        lax.psum_scatter(segment_grads[9], "dp", scatter_dimension=0, tiled=True),
        lax.psum_scatter(segment_grads[10], "dp", scatter_dimension=0, tiled=True),
        lax.psum_scatter(segment_grads[11], "dp", scatter_dimension=0, tiled=True),
        lax.psum_scatter(segment_grads[12], "dp", scatter_dimension=0, tiled=True),
        lax.psum_scatter(segment_grads[13], "dp", scatter_dimension=0, tiled=True),
        lax.psum_scatter(segment_grads[14], "dp", scatter_dimension=0, tiled=True),
        lax.psum_scatter(cross_grads[0], "dp", scatter_dimension=0, tiled=True),
        lax.psum_scatter(cross_grads[1], "dp", scatter_dimension=0, tiled=True),
        lax.psum_scatter(cross_grads[2], "dp", scatter_dimension=0, tiled=True),
        lax.psum_scatter(cross_grads[3], "dp", scatter_dimension=0, tiled=True),
        lax.psum_scatter(cross_grads[4], "dp", scatter_dimension=0, tiled=True),
        lax.psum_scatter(cross_grads[5], "dp", scatter_dimension=0, tiled=True),
        lax.psum_scatter(cross_grads[6], "dp", scatter_dimension=0, tiled=True),
        lax.psum_scatter(cross_grads[7], "dp", scatter_dimension=0, tiled=True),
        lax.psum_scatter(cross_grads[8], "dp", scatter_dimension=0, tiled=True),
        lax.psum_scatter(cross_grads[9], "dp", scatter_dimension=0, tiled=True),
        lax.psum_scatter(cross_grads[10], "dp", scatter_dimension=0, tiled=True),
        lax.psum_scatter(cross_grads[11], "dp", scatter_dimension=0, tiled=True),
        lax.psum_scatter(cross_grads[12], "dp", scatter_dimension=0, tiled=True),
        lax.psum_scatter(cross_grads[13], "dp", scatter_dimension=0, tiled=True),
        lax.psum_scatter(cross_grads[14], "dp", scatter_dimension=0, tiled=True),
        lax.psum_scatter(embed_grad, "dp", scatter_dimension=1, tiled=True),
    )
    summed = lax.psum(
        (
            shares[0],
            shares[1],
            shares[2],
            shares[3],
            shares[4],
            shares[5],
            shares[6],
            shares[7],
            shares[8],
            shares[9],
            shares[10],
            shares[11],
            shares[12],
            shares[13],
            shares[14],
            shares[15],
            shares[16],
            shares[17],
            shares[18],
            shares[19],
            shares[20],
            shares[21],
            shares[22],
            shares[23],
            shares[24],
            shares[25],
            shares[26],
            shares[27],
            shares[28],
            shares[29],
            shares[30],
        ),
        "seg",
    )
    totals = tuple((jnp.stack([summed[index], summed[index + 15]]) for index in range(15)))
    totals = totals + (summed[30],)
    return (output, input_grad) + tuple(totals)


def solution(mesh):
    placed = (
        P("dp", "seg", None),
        P("dp", None),
        P("dp", "seg", None),
        P(None, "dp", None),
        P(),
        P(None, "dp", None),
        P(None, "dp", None),
        P(),
        P(None, "dp", None),
        P(),
        P(),
        P(),
        P(None, "dp", None),
        P(),
        P(None, "dp", None),
        P(),
        P(),
        P(),
        P(),
    )
    return jax.shard_map(
        shards,
        mesh=mesh,
        in_specs=placed,
        out_specs=(
            P("dp", "seg", None),
            P("dp", "seg", None),
            P(None, "dp", None),
            P(None, "dp"),
            P(None, "dp", None),
            P(None, "dp", None),
            P(None, "dp"),
            P(None, "dp", None),
            P(None, "dp"),
            P(None, "dp"),
            P(None, "dp"),
            P(None, "dp", None),
            P(None, "dp"),
            P(None, "dp", None),
            P(None, "dp"),
            P(None, "dp"),
            P(None, "dp"),
            P(None, "dp"),
        ),
        check_vma=False,
    )
```

profile of v0, /device:TPU:0, one launch (start us, length us, event | category | flops | bytes accessed | tf_op | source)
XLA Modules:
  0.0 1615.4 jit_solution(5747079479511893777)
XLA Ops:
  11.4 15.6 all-gather.1
  32.1 17.8 %all-gather.10.cloned.1.call-done = bf16[2,768,768]{2,1,0:T(8,128)(2,1)} async-done(((bf16[2,192,768]{2,1,0:T(8,128)(2,1)}), bf16[2,768,768]{2,1,0:T(8,128)(2,1)}) %all-gather.10.cloned.1.call-update) | async-done | bytes 2359312 | tf_op jit(solution)/shard_map/all_gather | solution.py:242
  53.2 36.0 %all-gather.12.cloned.1.call-done = bf16[2,768,768]{2,1,0:T(8,128)(2,1)} async-done(((bf16[2,192,768]{2,1,0:T(8,128)(2,1)}), bf16[2,768,768]{2,1,0:T(8,128)(2,1)}) %all-gather.12.cloned.1.call-update) | async-done | bytes 2359312 | tf_op jit(solution)/shard_map/all_gather | solution.py:240
  91.6 36.8 %all-gather.14.cloned.1.call-done = bf16[2,768,768]{2,1,0:T(8,128)(2,1)} async-done(((bf16[2,192,768]{2,1,0:T(8,128)(2,1)}), bf16[2,768,768]{2,1,0:T(8,128)(2,1)}) %all-gather.14.cloned.1.call-update) | async-done | bytes 2359312 | tf_op jit(solution)/shard_map/all_gather | solution.py:241
  130.8 2.9 fusion.106
  133.8 2.7 convolution_convert_fusion.5
  136.5 31.0 %all-gather.16.cloned.1.call-done = bf16[2,768,768]{2,1,0:T(8,128)(2,1)} async-done(((bf16[2,192,768]{2,1,0:T(8,128)(2,1)}), bf16[2,768,768]{2,1,0:T(8,128)(2,1)}) %all-gather.16.cloned.1.call-update) | async-done | bytes 2359312 | tf_op jit(solution)/shard_map/all_gather | solution.py:243
  167.5 2.2 fusion.107
  170.0 95.4 %all-gather.18.cloned.1.call-done = bf16[2,768,3072]{2,1,0:T(8,128)(2,1)} async-done(((bf16[2,192,3072]{2,1,0:T(8,128)(2,1)}), bf16[2,768,3072]{2,1,0:T(8,128)(2,1)}) %all-gather.18.cloned.1.call-update) | async-done | bytes 9437200 | tf_op jit(solution)/shard_map/all_gather | solution.py:244
  265.4 6.9 fusion.33
  272.3 3.3 copy-done.7
  275.6 15.7 multiply_convert_fusion
  291.3 72.1 %all-gather.20.cloned.1.call-done = bf16[2,3072,768]{2,1,0:T(8,128)(2,1)} async-done(((bf16[2,768,768]{2,1,0:T(8,128)(2,1)}), bf16[2,3072,768]{2,1,0:T(8,128)(2,1)}) %all-gather.20.cloned.1.call-update) | async-done | bytes 9437200 | tf_op jit(solution)/shard_map/all_gather | solution.py:245
  363.3 6.0 fusion.108
  372.5 14.1 all-gather.2
  390.8 2.2 fusion.48
  400.7 3.4 fusion.22
  404.2 4.5 fusion.46
  412.1 2.4 convert_reduce_fusion.5
  423.3 2.4 convert_reduce_fusion.6
  439.2 9.9 multiply_reduce_fusion.1
  450.6 8.9 convert_reduce_fusion
  459.6 3.6 multiply_reduce_fusion.2
  467.9 3.2 convert_reduce_fusion.3
  472.0 2.2 convolution_bitcast_fusion.3
  474.2 3.1 copy.176
  478.4 2.9 fusion.25
  484.0 2.2 convolution_bitcast_fusion.5
  486.1 3.0 copy.168
  489.5 2.4 multiply_convert_fusion.1
  492.7 2.2 convolution_bitcast_fusion.4
  494.9 3.1 copy.172
  499.4 2.2 convolution_bitcast_fusion.2
  501.7 2.8 convolution_multiply_fusion.2
  510.6 7.2 convolution_bitcast_fusion.1
  519.8 6.2 convolution_bitcast_fusion
  527.0 5.9 convolution_multiply_fusion
  533.8 5.0 convolution_multiply_fusion.1
  549.8 2.2 copy.177
  552.0 3.3 reduce-scatter.40.cloned.1.call-done
  555.3 2.2 copy.169
  557.5 38.3 %reduce-scatter.44.cloned.1.call-done = f32[192,768]{1,0:T(8,128)} async-done(((f32[768,768]{1,0:T(8,128)}), f32[192,768]{1,0:T(8,128)}) %reduce-scatter.44.cloned.1.call-update) | async-done | bytes 589840
  595.7 2.2 copy.173
  598.0 38.1 %reduce-scatter.52.cloned.1.call-done = f32[192,768]{1,0:T(8,128)} async-done(((f32[768,768]{1,0:T(8,128)}), f32[192,768]{1,0:T(8,128)}) %reduce-scatter.52.cloned.1.call-update) | async-done | bytes 589840
  636.1 2.2 copy.181
  638.3 38.2 %reduce-scatter.54.cloned.1.call-done = f32[192,768]{1,0:T(8,128)} async-done(((f32[768,768]{1,0:T(8,128)}), f32[192,768]{1,0:T(8,128)}) %reduce-scatter.54.cloned.1.call-update) | async-done | bytes 589840
  676.5 2.2 copy.183
  678.8 38.1 %reduce-scatter.50.cloned.1.call-done = f32[192,768]{1,0:T(8,128)} async-done(((f32[768,768]{1,0:T(8,128)}), f32[192,768]{1,0:T(8,128)}) %reduce-scatter.50.cloned.1.call-update) | async-done | bytes 589840
  716.9 2.2 copy.179
  719.1 38.8 %reduce-scatter.42.cloned.1.call-done = f32[192,768]{1,0:T(8,128)} async-done(((f32[768,768]{1,0:T(8,128)}), f32[192,768]{1,0:T(8,128)}) %reduce-scatter.42.cloned.1.call-update) | async-done | bytes 589840
  757.9 2.2 copy.171
  760.1 38.1 %reduce-scatter.46.cloned.1.call-done = f32[192,768]{1,0:T(8,128)} async-done(((f32[768,768]{1,0:T(8,128)}), f32[192,768]{1,0:T(8,128)}) %reduce-scatter.46.cloned.1.call-update) | async-done | bytes 589840
  798.2 2.2 copy.175
  800.4 95.7 %reduce-scatter.32.cloned.1.call-done = f32[192,3072]{1,0:T(8,128)} async-done(((f32[768,3072]{1,0:T(8,128)}), f32[192,3072]{1,0:T(8,128)}) %reduce-scatter.32.cloned.1.call-update) | async-done | bytes 2359312 | tf_op jit(solution)/shard_map/reduce_scatter | solution.py:311
  896.1 97.9 %reduce-scatter.36.cloned.1.call-done = f32[768,768]{1,0:T(8,128)} async-done(((f32[3072,768]{1,0:T(8,128)}), f32[768,768]{1,0:T(8,128)}) %reduce-scatter.36.cloned.1.call-update) | async-done | bytes 2359312 | tf_op jit(solution)/shard_map/reduce_scatter | solution.py:313
  994.0 97.9 %reduce-scatter.38.cloned.1.call-done = f32[768,768]{1,0:T(8,128)} async-done(((f32[3072,768]{1,0:T(8,128)}), f32[768,768]{1,0:T(8,128)}) %reduce-scatter.38.cloned.1.call-update) | async-done | bytes 2359312 | tf_op jit(solution)/shard_map/reduce_scatter | solution.py:328
  1091.9 97.9 %reduce-scatter.34.cloned.1.call-done = f32[192,3072]{1,0:T(8,128)} async-done(((f32[768,3072]{1,0:T(8,128)}), f32[192,3072]{1,0:T(8,128)}) %reduce-scatter.34.cloned.1.call-update) | async-done | bytes 2359312 | tf_op jit(solution)/shard_map/reduce_scatter | solution.py:326
  1194.3 2.2 fusion.50
  1200.1 44.1 %all-reduce.26.cloned.1.call-done = (f32[768]{0:T(1024)}, f32[768]{0:T(1024)}, f32[768]{0:T(1024)}, f32[768]{0:T(1024)}, f32[768]{0:T(1024)}, /*index=5*/f32[768...) async-done(((f32[768]{0:T(1024)}, f32[768]{0:T(1024)}, ...) | async-done | bytes 73744
  1257.8 13.8 reduce-scatter.56.cloned.1.call-done
  1272.6 30.8 %all-reduce.18 = (f32[1,192]{1,0:T(1,128)S(1)}, f32[1,192]{1,0:T(1,128)S(1)}, f32[1,192]{1,0:T(1,128)S(1)}, f32[1,192]{1,0:T(1,128)S(1)}, f32[1,192]{1,0:T(1,128...) all-reduce(f32[1,192]{1,0:T(1,128)S(1)} %bitcast.354, ...), channel_id=1, replica_groups=mesh['dp'=4,'seg'=8] {'seg'}, use_global_device_ids=true, to_apply=%region_31.32 | all-reduce | flops 10752 | bytes 86016 | tf_op jit(solution)/shard_map/psum | solution.py:334
  1308.7 282.4 %all-reduce.24.cloned.1.call-done = (f32[1,192,768]{1,2,0:T(8,128)}, f32[1,192,768]{1,2,0:T(8,128)}, f32[1,192,768]{1,2,0:T(8,128)}, f32[1,192,768]{1,2,0:T(8,12...) async-done(((f32[1,192,768]{1,2,0:T(8,128)}, ...) | async-done | bytes 14155792 | tf_op jit(solution)/shard_map/psum | solution.py:334
  1600.4 5.2 pad_maximum_fusion
  1605.6 2.5 pad_maximum_fusion.1
  (418 shorter events, 127.5 us)
Async XLA Ops:
  7.2 42.8 %all-gather.10.cloned.1.call-start = ((), (), s32[]{:S(2)}) async-start(), calls=%async_computation.13 | async-start | bytes 2949120 | tf_op jit(solution)/shard_map/all_gather | solution.py:242
  7.9 81.2 %all-gather.12.cloned.1.call-start = ((), (), s32[]{:S(2)}) async-start(), calls=%async_computation.14 | async-start | bytes 2949120 | tf_op jit(solution)/shard_map/all_gather | solution.py:240
  8.7 119.7 %all-gather.14.cloned.1.call-start = ((), (), s32[]{:S(2)}) async-start(), calls=%async_computation.15 | async-start | bytes 2949120 | tf_op jit(solution)/shard_map/all_gather | solution.py:241
  9.4 158.0 %all-gather.16.cloned.1.call-start = ((), (), s32[]{:S(2)}) async-start(), calls=%async_computation.16 | async-start | bytes 2949120 | tf_op jit(solution)/shard_map/all_gather | solution.py:243
  10.0 17.0 %copy-start.83 = (bf16[2,768]{1,0:T(2,128)(2,1)S(1)}, bf16[2,768]{1,0:T(2,128)(2,1)}, u32[]{:S(2)}) copy-start(bf16[2,768]{1,0:T(2,128)(2,1)} %param.23) | copy-start | bytes 9220
  10.0 17.0 %copy-start.84 = (bf16[2,768]{1,0:T(2,128)(2,1)S(1)}, bf16[2,768]{1,0:T(2,128)(2,1)}, u32[]{:S(2)}) copy-start(bf16[2,768]{1,0:T(2,128)(2,1)} %param.26) | copy-start | bytes 9220
  10.0 17.0 %copy-start.85 = (bf16[2,768]{1,0:T(2,128)(2,1)S(1)}, bf16[2,768]{1,0:T(2,128)(2,1)}, u32[]{:S(2)}) copy-start(bf16[2,768]{1,0:T(2,128)(2,1)} %param.28) | copy-start | bytes 9220
  10.0 17.6 %copy-start.86 = (bf16[2,768]{1,0:T(2,128)(2,1)S(1)}, bf16[2,768]{1,0:T(2,128)(2,1)}, u32[]{:S(2)}) copy-start(bf16[2,768]{1,0:T(2,128)(2,1)} %param.29) | copy-start | bytes 9220
  10.0 18.2 %copy-start.87 = (bf16[2,768]{1,0:T(2,128)(2,1)S(1)}, bf16[2,768]{1,0:T(2,128)(2,1)}, u32[]{:S(2)}) copy-start(bf16[2,768]{1,0:T(2,128)(2,1)} %param.34) | copy-start | bytes 9220
  10.1 18.2 %copy-start.88 = (bf16[2,768]{1,0:T(2,128)(2,1)S(1)}, bf16[2,768]{1,0:T(2,128)(2,1)}, u32[]{:S(2)}) copy-start(bf16[2,768]{1,0:T(2,128)(2,1)} %param.30) | copy-start | bytes 9220
  10.1 18.8 %copy-start.89 = (bf16[2,768]{1,0:T(2,128)(2,1)S(1)}, bf16[2,768]{1,0:T(2,128)(2,1)}, u32[]{:S(2)}) copy-start(bf16[2,768]{1,0:T(2,128)(2,1)} %param.36) | copy-start | bytes 9220
  10.1 18.8 %copy-start.90 = (bf16[2,768]{1,0:T(2,128)(2,1)S(1)}, bf16[2,768]{1,0:T(2,128)(2,1)}, u32[]{:S(2)}) copy-start(bf16[2,768]{1,0:T(2,128)(2,1)} %param.35) | copy-start | bytes 9220
  10.1 19.5 %copy-start.99 = (s32[1,32]{1,0:T(1,128)S(1)}, s32[1,32]{1,0:T(1,128)}, u32[]{:S(2)}) copy-start(s32[1,32]{1,0:T(1,128)} %param.20) | copy-start | bytes 388
  10.1 255.3 %all-gather.18.cloned.1.call-start = ((), (), s32[]{:S(2)}) async-start(), calls=%async_computation.17 | async-start | bytes 11796480 | tf_op jit(solution)/shard_map/all_gather | solution.py:244
  10.7 20.8 %copy-start.66 = (bf16[2,3072]{1,0:T(2,128)(2,1)S(1)}, bf16[2,3072]{1,0:T(2,128)(2,1)}, u32[]{:S(2)}) copy-start(bf16[2,3072]{1,0:T(2,128)(2,1)} %param.32) | copy-start | bytes 36868
  10.7 39.3 %copy-start.3 = (bf16[1,512,768]{2,1,0:T(8,128)(2,1)S(1)}, bf16[1,512,768]{2,1,0:T(8,128)(2,1)}, u32[]{:S(2)}) copy-start(bf16[1,512,768]{2,1,0:T(8,128)(2,1)} %param.19) | copy-start | bytes 2359300
  10.7 352.6 %all-gather.20.cloned.1.call-start = ((), (), s32[]{:S(2)}) async-start(), calls=%async_computation.18 | async-start | bytes 11796480 | tf_op jit(solution)/shard_map/all_gather | solution.py:245
  11.3 538.5 %reduce-scatter.48.cloned.1.call-start = ((), (), s32[]{:S(2)}) async-start(), calls=%async_computation.27 | async-start | bytes 2949120
  28.3 335.1 %copy-start.81 = (f32[768]{0:T(1024)}, f32[768]{0:T(1024)S(1)}, u32[]{:S(2)}) copy-start(f32[768]{0:T(1024)S(1)} %get-tuple-element.91) | copy-start | bytes 9220
  28.9 334.4 %copy-start.96 = (f32[768]{0:T(1024)}, f32[768]{0:T(1024)S(1)}, u32[]{:S(2)}) copy-start(f32[768]{0:T(1024)S(1)} %get-tuple-element.207) | copy-start | bytes 9220
  29.5 340.7 %copy-start.58 = (f32[768]{0:T(1024)}, f32[768]{0:T(1024)S(1)}, u32[]{:S(2)}) copy-start(f32[768]{0:T(1024)S(1)} %get-tuple-element.209) | copy-start | bytes 9220
  32.1 240.2 %copy-start.64 = (f32[1,3072]{1,0:T(1,128)}, f32[1,3072]{1,0:T(1,128)S(1)}, u32[]{:S(2)}) copy-start(f32[1,3072]{1,0:T(1,128)S(1)} %get-tuple-element.178) | copy-start | bytes 36868
  91.6 39.2 %copy-start.14 = (bf16[4,128,768]{1,2,0:T(8,128)(2,1)}, bf16[4,128,768]{1,2,0:T(8,128)(2,1)S(1)}, u32[]{:S(2)}) copy-start(bf16[4,128,768]{1,2,0:T(8,128)(2,1)S(1)} %copy.115) | copy-start | bytes 2359300
  136.5 33.5 %copy-start.17 = (bf16[4,12,64,128]{3,2,1,0:T(8,128)(2,1)}, bf16[4,12,64,128]{3,2,1,0:T(8,128)(2,1)S(1)}, u32[]{:S(2)}) copy-start(bf16[4,12,64,128]{3,2,1,0:T(8,128)(2,1)S(1)} %convolution_convert_fusion.5) | copy-start | bytes 2359300
  169.7 193.7 %copy-start.71 = (f32[4,128]{1,0:T(4,128)}, f32[4,128]{1,0:T(4,128)S(1)}, u32[]{:S(2)}) copy-start(f32[4,128]{1,0:T(4,128)S(1)} %broadcast_multiply_fusion.11) | copy-start | bytes 6148
  170.0 95.4 %copy-start.73 = (f32[4,128]{1,0:T(4,128)}, f32[4,128]{1,0:T(4,128)S(1)}, u32[]{:S(2)}) copy-start(f32[4,128]{1,0:T(4,128)S(1)} %multiply_reduce_fusion.6) | copy-start | bytes 6148
  170.0 193.3 %copy-start.93 = (f32[4,128]{1,0:T(4,128)}, f32[4,128]{1,0:T(4,128)S(1)}, u32[]{:S(2)}) copy-start(f32[4,128]{1,0:T(4,128)S(1)} %fusion.95) | copy-start | bytes 6148
  388.3 7.8 copy-start.46
  400.7 11.4 copy-start.101
  404.2 7.9 copy-start.50
  404.2 10.3 slice-start.2
  404.2 10.3 slice-start.3
  417.2 9.6 copy-start.47
  417.8 9.9 copy-start.100
  431.1 8.0 copy-start.59
  431.1 8.0 copy-start.63
  431.1 8.0 copy-start.70
  431.9 7.3 copy-start
  431.9 18.7 %slice-start = ((s8[6291456]{0:T(1024)(128)(4,1)}), s8[4194304]{0:T(1024)(128)(4,1)S(1)}, s32[]{:S(2)}) async-start(s8[6291456]{0:T(1024)(128)(4,1)} %bitcast.309), calls=%async_computation.34 | async-start | bytes 8388608
  435.7 13.3 copy-start.76
  439.2 11.4 slice-start.1
  449.8 9.8 slice-start.5
  450.6 9.0 copy-start.37
  450.6 8.9 slice-start.6
  450.6 8.9 slice-start.7
  450.6 8.9 copy-start.72
  450.6 8.9 copy-start.82
  450.6 8.9 copy-start.94
  477.3 78.0 %reduce-scatter.40.cloned.1.call-start = ((), (), s32[]{:S(2)}) async-start(), calls=%async_computation.23 | async-start | bytes 2949120
  489.2 106.6 %reduce-scatter.44.cloned.1.call-start = ((), (), s32[]{:S(2)}) async-start(), calls=%async_computation.25 | async-start | bytes 2949120
  498.1 138.0 %reduce-scatter.52.cloned.1.call-start = ((), (), s32[]{:S(2)}) async-start(), calls=%async_computation.29 | async-start | bytes 2949120
  501.7 174.9 %reduce-scatter.54.cloned.1.call-start = ((), (), s32[]{:S(2)}) async-start(), calls=%async_computation.30 | async-start | bytes 2949120
  504.6 212.3 %reduce-scatter.50.cloned.1.call-start = ((), (), s32[]{:S(2)}) async-start(), calls=%async_computation.28 | async-start | bytes 2949120
  506.6 251.3 %reduce-scatter.42.cloned.1.call-start = ((), (), s32[]{:S(2)}) async-start(), calls=%async_computation.24 | async-start | bytes 2949120
  508.6 289.6 %reduce-scatter.46.cloned.1.call-start = ((), (), s32[]{:S(2)}) async-start(), calls=%async_computation.26 | async-start | bytes 2949120
  510.6 385.5 %reduce-scatter.32.cloned.1.call-start = ((), (), s32[]{:S(2)}) async-start(), calls=%async_computation.19 | async-start | bytes 11796480 | tf_op jit(solution)/shard_map/reduce_scatter | solution.py:311
  517.9 476.1 %reduce-scatter.36.cloned.1.call-start = ((), (), s32[]{:S(2)}) async-start(), calls=%async_computation.21 | async-start | bytes 11796480 | tf_op jit(solution)/shard_map/reduce_scatter | solution.py:313
  526.0 565.9 %reduce-scatter.38.cloned.1.call-start = ((), (), s32[]{:S(2)}) async-start(), calls=%async_computation.22 | async-start | bytes 11796480 | tf_op jit(solution)/shard_map/reduce_scatter | solution.py:328
  532.9 656.9 %reduce-scatter.34.cloned.1.call-start = ((), (), s32[]{:S(2)}) async-start(), calls=%async_computation.20 | async-start | bytes 11796480 | tf_op jit(solution)/shard_map/reduce_scatter | solution.py:326
  538.9 8.3 copy-start.79
  538.9 8.9 copy-start.91
  538.9 705.3 %all-reduce.26.cloned.1.call-start = ((), (), s32[]{:S(2)}) async-start(), calls=%async_computation.33 | async-start | bytes 180224
  548.4 723.2 %reduce-scatter.56.cloned.1.call-start = ((), (), s32[]{:S(2)}) async-start(), calls=%async_computation.31 | async-start | bytes 491520
  549.5 1041.6 %all-reduce.24.cloned.1.call-start = ((), (), s32[]{:S(2)}) async-start(), calls=%async_computation.32 | async-start | bytes 31457280 | tf_op jit(solution)/shard_map/psum | solution.py:334
  (69 other events, 177.7 us)
Sparse Core Ops, SparseCore 0:
  9.8 40.0 all-gather.9
  51.8 37.3 all-gather.11
  91.0 37.3 all-gather.13
  130.1 37.3 all-gather.15
  169.1 96.1 all-gather.17
  267.1 96.1 all-gather.19
  477.4 37.3 reduce-scatter.47
  517.9 37.3 reduce-scatter.39
  558.3 37.3 reduce-scatter.43
  598.6 37.3 reduce-scatter.51
  639.1 37.3 reduce-scatter.53
  679.4 37.3 reduce-scatter.49
  720.5 37.3 reduce-scatter.41
  760.8 37.3 reduce-scatter.45
  801.2 94.8 reduce-scatter.31
  899.1 94.8 reduce-scatter.35
  997.0 94.8 reduce-scatter.37
  1094.8 94.8 reduce-scatter.33
  1195.7 48.4 all-reduce.25
  1246.9 24.6 reduce-scatter.55
  1276.2 314.8 all-reduce.23
where the time goes:
time: 1630 us; the launch traced here: 1620 us
  waiting for transfers between devices  1260 us (77%)
  matrix products  130 us (8%)
  local copies, waits for them, and re-layouts  81.8 us (5%)
  other arithmetic  69.1 us (4%)
  blocking collectives  60.5 us (4%)
  between operations  17.4 us (1%)
    unnamed x31, waiting for transfers between devices  295 us
    psum x1, waiting for transfers between devices, shards(): lax.psum((shares[0], shares[1], shares[2], shares[3], shares[4], shares[5...  282 us
    reduce_scatter x1, waiting for transfers between devices, shards(): lax.psum_scatter(cross_grads[9], 'dp', scatter_dimension=0, tiled=True)  97.9 us
    reduce_scatter x1, waiting for transfers between devices, shards(): lax.psum_scatter(segment_grads[11], 'dp', scatter_dimension=0, tiled=True)  97.9 us
    reduce_scatter x1, waiting for transfers between devices, shards(): lax.psum_scatter(cross_grads[11], 'dp', scatter_dimension=0, tiled=True)  97.9 us
    reduce_scatter x1, waiting for transfers between devices, shards(): lax.psum_scatter(segment_grads[9], 'dp', scatter_dimension=0, tiled=True)  95.7 us
    all_gather x1, waiting for transfers between devices, shards(): lax.all_gather(inner_weight, 'dp', axis=1, tiled=True)  95.4 us
    all_gather x1, waiting for transfers between devices, shards(): lax.all_gather(outer_weight, 'dp', axis=1, tiled=True)  72.1 us
  transfers between devices with their start and end apart: 21, of which 20 were waited for; matrix products, arithmetic and copies ran while one was open for 9% of the time, Pallas kernels for 0%

commit v1 on v0

--- a/solution.py
+++ b/solution.py
@@ -7,6 +7,22 @@
 HEAD_DIM = 64
 SEG_LEN = 128
 epsilon = 1e-05
+
+
+def gather_around(x, axis, dim):
+    ways, here, step = (lax.axis_size(axis), lax.axis_index(axis), x.shape[dim])
+    shape = [n * ways if d == dim else n for d, n in enumerate(x.shape)]
+    full = lax.dynamic_update_slice_in_dim(jnp.zeros(shape, x.dtype), x, here * step, axis=dim)
+    going_up = going_down = x
+    for far in range(1, ways // 2 + 1):
+        going_up = lax.ppermute(going_up, axis, [(d, (d + 1) % ways) for d in range(ways)])
+        full = lax.dynamic_update_slice_in_dim(full, going_up, (here - far) % ways * step, axis=dim)
+        if 2 * far < ways:
+            going_down = lax.ppermute(going_down, axis, [(d, (d - 1) % ways) for d in range(ways)])
+            full = lax.dynamic_update_slice_in_dim(
+                full, going_down, (here + far) % ways * step, axis=dim
+            )
+    return full
 
 
 def normalize(values, gain, shift):
@@ -238,7 +254,7 @@
     seg_local = local_length // SEG_LEN
     query_full, key_full, value_full, out_full, inner_full, outer_full = (
         lax.all_gather(query_weight, "dp", axis=1, tiled=True),
-        lax.all_gather(key_weight, "dp", axis=1, tiled=True),
+        gather_around(key_weight, "dp", 1),
         lax.all_gather(value_weight, "dp", axis=1, tiled=True),
         lax.all_gather(out_weight, "dp", axis=1, tiled=True),
         lax.all_gather(inner_weight, "dp", axis=1, tiled=True),

time: 1630 us -> 1590 us (0.975)
  waiting for transfers between devices: 1260 us -> 1190 us
  local copies, waits for them, and re-layouts: 81.8 us -> 123 us
    all_gather x1 -> x0, waiting for transfers between devices: 36.8 us -> none  [shards(): lax.all_gather(key_weight, 'dp', axis=1, tiled=True)]
    dynamic_update_slice x0 -> x4, local copies, waits for them, and re-layouts: none -> 33.5 us  [the longest x2 14.8 us: gather_around(): lax.dynamic_update_slice_in_dim(full, going_up, (here - far) % ways * ste...]
    all_gather x1, waiting for transfers between devices: 36 us -> 14.6 us  [shards(): lax.all_gather(query_weight, 'dp', axis=1, tiled=True)]
    all_gather x1, waiting for transfers between devices: 17.8 us -> 0.01 us  [shards(): lax.all_gather(value_weight, 'dp', axis=1, tiled=True)]
    unnamed x261 -> x270, local copies, waits for them, and re-layouts: 68.9 us -> 72.5 us
    unnamed x31 -> x30, waiting for transfers between devices: 295 us -> 297 us
  transfers between devices with their start and end apart: 21 -> 23, of which waited for: 20 -> 19; matrix products, arithmetic and copies ran while one was open for 9% -> 12% of each run, Pallas kernels for 0% -> 0%
where the time goes in v1:
time: 1590 us
  waiting for transfers between devices  1190 us (75%)
  matrix products  133 us (8%)
  local copies, waits for them, and re-layouts  123 us (8%)
  other arithmetic  60.5 us (4%)
  blocking collectives  59 us (4%)
  between operations  17.2 us (1%)
    unnamed x30, waiting for transfers between devices  297 us
    psum x1, waiting for transfers between devices, shards(): lax.psum((shares[0], shares[1], shares[2], shares[3], shares[4], shares[5...  282 us
    reduce_scatter x1, waiting for transfers between devices, shards(): lax.psum_scatter(cross_grads[11], 'dp', scatter_dimension=0, tiled=True)  97.9 us
    reduce_scatter x1, waiting for transfers between devices, shards(): lax.psum_scatter(cross_grads[9], 'dp', scatter_dimension=0, tiled=True)  97.9 us
    reduce_scatter x1, waiting for transfers between devices, shards(): lax.psum_scatter(segment_grads[11], 'dp', scatter_dimension=0, tiled=True)  97.9 us
    reduce_scatter x1, waiting for transfers between devices, shards(): lax.psum_scatter(segment_grads[9], 'dp', scatter_dimension=0, tiled=True)  95.7 us
    all_gather x1, waiting for transfers between devices, shards(): lax.all_gather(inner_weight, 'dp', axis=1, tiled=True)  95.4 us
    unnamed x270, local copies, waits for them, and re-layouts  72.5 us
  transfers between devices with their start and end apart: 23, of which 19 were waited for; matrix products, arithmetic and copies ran while one was open for 12% of the time, Pallas kernels for 0%

profile of v1, /device:TPU:0, one launch (start us, length us, event | category | flops | bytes accessed | tf_op | source)
XLA Modules:
  0.0 1588.6 jit_solution(3591553660387424964)
XLA Ops:
  10.6 4.0 collective-permute-start.1
  14.6 2.3 copy.121
  17.2 9.7 dynamic_update_slice.12
  26.9 14.1 all-gather.1
  45.6 7.4 collective-permute-done
  53.0 2.6 collective-permute-start.2
  57.6 7.1 dynamic_update_slice.13
  67.4 9.0 dynamic_update_slice.14
  77.8 7.7 dynamic_update_slice.15
  85.6 3.0 convolution_convert_fusion.3
  91.0 14.6 all-gather.11.cloned.1.call-done
  108.1 4.3 fusion.106
  112.4 2.6 convolution_convert_fusion.5
  115.0 29.8 %all-gather.13.cloned.1.call-done = bf16[2,768,768]{2,1,0:T(8,128)(2,1)} async-done(((bf16[2,192,768]{2,1,0:T(8,128)(2,1)}), bf16[2,768,768]{2,1,0:T(8,128)(2,1)}) %all-gather.13.cloned.1.call-update) | async-done | bytes 2359312 | tf_op jit(solution)/shard_map/all_gather | solution.py:259
  147.4 95.4 %all-gather.15.cloned.1.call-done = bf16[2,768,3072]{2,1,0:T(8,128)(2,1)} async-done(((bf16[2,192,3072]{2,1,0:T(8,128)(2,1)}), bf16[2,768,3072]{2,1,0:T(8,128)(2,1)}) %all-gather.15.cloned.1.call-update) | async-done | bytes 9437200 | tf_op jit(solution)/shard_map/all_gather | solution.py:260
  242.8 6.9 fusion.33
  249.7 3.3 copy-done.11
  252.9 15.8 multiply_convert_fusion
  268.8 71.9 %all-gather.17.cloned.1.call-done = bf16[2,3072,768]{2,1,0:T(8,128)(2,1)} async-done(((bf16[2,768,768]{2,1,0:T(8,128)(2,1)}), bf16[2,3072,768]{2,1,0:T(8,128)(2,1)}) %all-gather.17.cloned.1.call-update) | async-done | bytes 9437200 | tf_op jit(solution)/shard_map/all_gather | solution.py:261
  340.7 6.0 fusion.108
  349.9 14.1 all-gather.2
  368.3 2.2 fusion.48
  378.3 3.4 fusion.22
  381.8 4.6 fusion.46
  389.6 2.4 convert_reduce_fusion.5
  400.8 2.4 convert_reduce_fusion.6
  406.0 2.3 fusion.53
  420.1 8.7 convert_reduce_fusion
  428.8 3.6 multiply_reduce_fusion.2
  439.1 3.0 fusion.25
  447.6 3.1 copy.183
  455.7 3.0 copy.179
  459.9 3.2 convert_reduce_fusion.3
  466.1 3.1 copy.187
  473.0 2.8 convolution_multiply_fusion.2
  481.9 7.2 convolution_bitcast_fusion.1
  491.0 6.2 convolution_bitcast_fusion
  498.4 5.8 convolution_multiply_fusion
  505.2 5.1 convolution_multiply_fusion.1
  521.2 2.2 copy.184
  523.4 5.3 reduce-scatter.40.cloned.1.call-done
  528.7 2.2 copy.180
  530.9 38.3 %reduce-scatter.48.cloned.1.call-done = f32[192,768]{1,0:T(8,128)} async-done(((f32[768,768]{1,0:T(8,128)}), f32[192,768]{1,0:T(8,128)}) %reduce-scatter.48.cloned.1.call-update) | async-done | bytes 589840
  569.2 2.3 copy.188
  571.4 38.2 %reduce-scatter.52.cloned.1.call-done = f32[192,768]{1,0:T(8,128)} async-done(((f32[768,768]{1,0:T(8,128)}), f32[192,768]{1,0:T(8,128)}) %reduce-scatter.52.cloned.1.call-update) | async-done | bytes 589840
  609.6 2.2 copy.192
  611.9 38.1 %reduce-scatter.54.cloned.1.call-done = f32[192,768]{1,0:T(8,128)} async-done(((f32[768,768]{1,0:T(8,128)}), f32[192,768]{1,0:T(8,128)}) %reduce-scatter.54.cloned.1.call-update) | async-done | bytes 589840
  650.0 2.3 copy.194
  652.2 38.2 %reduce-scatter.50.cloned.1.call-done = f32[192,768]{1,0:T(8,128)} async-done(((f32[768,768]{1,0:T(8,128)}), f32[192,768]{1,0:T(8,128)}) %reduce-scatter.50.cloned.1.call-update) | async-done | bytes 589840
  692.6 38.7 %reduce-scatter.42.cloned.1.call-done = f32[192,768]{1,0:T(8,128)} async-done(((f32[768,768]{1,0:T(8,128)}), f32[192,768]{1,0:T(8,128)}) %reduce-scatter.42.cloned.1.call-update) | async-done | bytes 589840
  731.3 2.2 copy.182
  733.5 38.3 %reduce-scatter.46.cloned.1.call-done = f32[192,768]{1,0:T(8,128)} async-done(((f32[768,768]{1,0:T(8,128)}), f32[192,768]{1,0:T(8,128)}) %reduce-scatter.46.cloned.1.call-update) | async-done | bytes 589840
  771.8 2.2 copy.186
  774.0 95.7 %reduce-scatter.32.cloned.1.call-done = f32[192,3072]{1,0:T(8,128)} async-done(((f32[768,3072]{1,0:T(8,128)}), f32[192,3072]{1,0:T(8,128)}) %reduce-scatter.32.cloned.1.call-update) | async-done | bytes 2359312 | tf_op jit(solution)/shard_map/reduce_scatter | solution.py:327
  869.7 97.9 %reduce-scatter.36.cloned.1.call-done = f32[768,768]{1,0:T(8,128)} async-done(((f32[3072,768]{1,0:T(8,128)}), f32[768,768]{1,0:T(8,128)}) %reduce-scatter.36.cloned.1.call-update) | async-done | bytes 2359312 | tf_op jit(solution)/shard_map/reduce_scatter | solution.py:329
  967.6 97.9 %reduce-scatter.38.cloned.1.call-done = f32[768,768]{1,0:T(8,128)} async-done(((f32[3072,768]{1,0:T(8,128)}), f32[768,768]{1,0:T(8,128)}) %reduce-scatter.38.cloned.1.call-update) | async-done | bytes 2359312 | tf_op jit(solution)/shard_map/reduce_scatter | solution.py:344
  1065.5 97.9 %reduce-scatter.34.cloned.1.call-done = f32[192,3072]{1,0:T(8,128)} async-done(((f32[768,3072]{1,0:T(8,128)}), f32[192,3072]{1,0:T(8,128)}) %reduce-scatter.34.cloned.1.call-update) | async-done | bytes 2359312 | tf_op jit(solution)/shard_map/reduce_scatter | solution.py:342
  1168.9 2.2 fusion.50
  1173.1 44.6 %all-reduce.26.cloned.1.call-done = (f32[768]{0:T(1024)}, f32[768]{0:T(1024)}, f32[768]{0:T(1024)}, f32[768]{0:T(1024)}, f32[768]{0:T(1024)}, /*index=5*/f32[768...) async-done(((f32[768]{0:T(1024)}, f32[768]{0:T(1024)}, ...) | async-done | bytes 73744
  1231.2 14.0 reduce-scatter.56.cloned.1.call-done
  1246.1 30.8 %all-reduce.18 = (f32[1,192]{1,0:T(1,128)S(1)}, f32[1,192]{1,0:T(1,128)S(1)}, f32[1,192]{1,0:T(1,128)S(1)}, f32[1,192]{1,0:T(1,128)S(1)}, f32[1,192]{1,0:T(1,128...) all-reduce(f32[1,192]{1,0:T(1,128)S(1)} %bitcast.356, ...), channel_id=1, replica_groups=mesh['dp'=4,'seg'=8] {'seg'}, use_global_device_ids=true, to_apply=%region_31.32 | all-reduce | flops 10752 | bytes 86016 | tf_op jit(solution)/shard_map/psum | solution.py:350
  1282.2 282.2 %all-reduce.24.cloned.1.call-done = (f32[1,192,768]{1,2,0:T(8,128)}, f32[1,192,768]{1,2,0:T(8,128)}, f32[1,192,768]{1,2,0:T(8,128)}, f32[1,192,768]{1,2,0:T(8,12...) async-done(((f32[1,192,768]{1,2,0:T(8,128)}, ...) | async-done | bytes 14155792 | tf_op jit(solution)/shard_map/psum | solution.py:350
  1573.7 5.2 pad_maximum_fusion
  1579.0 2.5 pad_maximum_fusion.1
  (436 shorter events, 146.1 us)
Async XLA Ops:
  7.2 81.4 %all-gather.9.cloned.1.call-start = ((), (), s32[]{:S(2)}) async-start(), calls=%async_computation.13 | async-start | bytes 2949120 | tf_op jit(solution)/shard_map/all_gather | solution.py:258
  7.9 97.7 %all-gather.11.cloned.1.call-start = ((), (), s32[]{:S(2)}) async-start(), calls=%async_computation.14 | async-start | bytes 2949120 | tf_op jit(solution)/shard_map/all_gather | solution.py:256
  8.7 136.2 %all-gather.13.cloned.1.call-start = ((), (), s32[]{:S(2)}) async-start(), calls=%async_computation.15 | async-start | bytes 2949120 | tf_op jit(solution)/shard_map/all_gather | solution.py:259
  9.4 233.4 %all-gather.15.cloned.1.call-start = ((), (), s32[]{:S(2)}) async-start(), calls=%async_computation.16 | async-start | bytes 11796480 | tf_op jit(solution)/shard_map/all_gather | solution.py:260
  10.0 330.7 %all-gather.17.cloned.1.call-start = ((), (), s32[]{:S(2)}) async-start(), calls=%async_computation.17 | async-start | bytes 11796480 | tf_op jit(solution)/shard_map/all_gather | solution.py:261
  10.6 510.6 %reduce-scatter.44.cloned.1.call-start = ((), (), s32[]{:S(2)}) async-start(), calls=%async_computation.24 | async-start | bytes 2949120
  10.6 54.1 %collective-permute-start.1 = (bf16[2,192,768]{2,1,0:T(8,128)(2,1)}, bf16[2,192,768]{2,1,0:T(8,128)(2,1)}, u32[]{:S(2)}, u32[]{:S(2)}) collective-permute-start(bf16[2,192,768]{2,1,0:T(8,128)(2,1)} %param.24), channel_id=1, source_target_pairs={{0,24},{8,0},{16,8},{24,16},{1,25},{9,1},{17,9},{25,17},{2,26},{10... | collective-permute-start | bytes 1769480 | tf_op jit(solution)/shard_map/ppermute | solution.py:21
  14.6 38.4 %collective-permute-start = (bf16[2,192,768]{2,1,0:T(8,128)(2,1)}, bf16[2,192,768]{2,1,0:T(8,128)(2,1)}, u32[]{:S(2)}, u32[]{:S(2)}) collective-permute-start(bf16[2,192,768]{2,1,0:T(8,128)(2,1)} %param.24), channel_id=1, source_target_pairs={{0,8},{8,16},{16,24},{24,0},{1,9},{9,17},{17,25},{25,1},{2,10},{10... | collective-permute-start | bytes 1769480 | tf_op jit(solution)/shard_map/ppermute | solution.py:18
  14.6 12.3 copy-start.14
  16.9 24.1 %copy-start.87 = (bf16[2,768]{1,0:T(2,128)(2,1)S(1)}, bf16[2,768]{1,0:T(2,128)(2,1)}, u32[]{:S(2)}) copy-start(bf16[2,768]{1,0:T(2,128)(2,1)} %param.23) | copy-start | bytes 9220
  16.9 24.2 %copy-start.88 = (bf16[2,768]{1,0:T(2,128)(2,1)S(1)}, bf16[2,768]{1,0:T(2,128)(2,1)}, u32[]{:S(2)}) copy-start(bf16[2,768]{1,0:T(2,128)(2,1)} %param.26) | copy-start | bytes 9220
  16.9 24.2 %copy-start.89 = (bf16[2,768]{1,0:T(2,128)(2,1)S(1)}, bf16[2,768]{1,0:T(2,128)(2,1)}, u32[]{:S(2)}) copy-start(bf16[2,768]{1,0:T(2,128)(2,1)} %param.28) | copy-start | bytes 9220
  16.9 24.8 %copy-start.90 = (bf16[2,768]{1,0:T(2,128)(2,1)S(1)}, bf16[2,768]{1,0:T(2,128)(2,1)}, u32[]{:S(2)}) copy-start(bf16[2,768]{1,0:T(2,128)(2,1)} %param.34) | copy-start | bytes 9220
  16.9 24.8 %copy-start.91 = (bf16[2,768]{1,0:T(2,128)(2,1)S(1)}, bf16[2,768]{1,0:T(2,128)(2,1)}, u32[]{:S(2)}) copy-start(bf16[2,768]{1,0:T(2,128)(2,1)} %param.30) | copy-start | bytes 9220
  16.9 25.4 %copy-start.92 = (bf16[2,768]{1,0:T(2,128)(2,1)S(1)}, bf16[2,768]{1,0:T(2,128)(2,1)}, u32[]{:S(2)}) copy-start(bf16[2,768]{1,0:T(2,128)(2,1)} %param.36) | copy-start | bytes 9220
  17.0 25.4 %copy-start.93 = (bf16[2,768]{1,0:T(2,128)(2,1)S(1)}, bf16[2,768]{1,0:T(2,128)(2,1)}, u32[]{:S(2)}) copy-start(bf16[2,768]{1,0:T(2,128)(2,1)} %param.35) | copy-start | bytes 9220
  17.0 26.0 %copy-start.94 = (bf16[2,768]{1,0:T(2,128)(2,1)S(1)}, bf16[2,768]{1,0:T(2,128)(2,1)}, u32[]{:S(2)}) copy-start(bf16[2,768]{1,0:T(2,128)(2,1)} %param.29) | copy-start | bytes 9220
  17.0 26.6 %copy-start.103 = (s32[1,32]{1,0:T(1,128)S(1)}, s32[1,32]{1,0:T(1,128)}, u32[]{:S(2)}) copy-start(s32[1,32]{1,0:T(1,128)} %param.20) | copy-start | bytes 388
  17.2 38.5 %copy-start.70 = (bf16[2,3072]{1,0:T(2,128)(2,1)S(1)}, bf16[2,3072]{1,0:T(2,128)(2,1)}, u32[]{:S(2)}) copy-start(bf16[2,3072]{1,0:T(2,128)(2,1)} %param.32) | copy-start | bytes 36868
  42.4 298.3 %copy-start.100 = (f32[768]{0:T(1024)}, f32[768]{0:T(1024)S(1)}, u32[]{:S(2)}) copy-start(f32[768]{0:T(1024)S(1)} %get-tuple-element.207) | copy-start | bytes 9220
  43.0 304.7 %copy-start.62 = (f32[768]{0:T(1024)}, f32[768]{0:T(1024)S(1)}, u32[]{:S(2)}) copy-start(f32[768]{0:T(1024)S(1)} %get-tuple-element.209) | copy-start | bytes 9220
  43.6 297.1 %copy-start.85 = (f32[768]{0:T(1024)}, f32[768]{0:T(1024)S(1)}, u32[]{:S(2)}) copy-start(f32[768]{0:T(1024)S(1)} %get-tuple-element.91) | copy-start | bytes 9220
  53.0 23.5 %collective-permute-start.2 = (bf16[2,192,768]{2,1,0:T(8,128)(2,1)}, bf16[2,192,768]{2,1,0:T(8,128)(2,1)}, u32[]{:S(2)}, u32[]{:S(2)}) collective-permute-start(bf16[2,192,768]{2,1,0:T(8,128)(2,1)} %collective-permute-done), channel_id=1, source_target_pairs={{0,8},{8,16},{16,24},{24,0},{1,9},{9,17},{17,25},{25,1},{2,10},{10... | collective-permute-start | bytes 1769480 | tf_op jit(solution)/shard_map/ppermute | solution.py:18
  56.2 193.4 %copy-start.68 = (f32[1,3072]{1,0:T(1,128)}, f32[1,3072]{1,0:T(1,128)S(1)}, u32[]{:S(2)}) copy-start(f32[1,3072]{1,0:T(1,128)S(1)} %get-tuple-element.178) | copy-start | bytes 36868
  67.4 18.2 %copy-start.3 = (bf16[1,512,768]{2,1,0:T(8,128)(2,1)S(1)}, bf16[1,512,768]{2,1,0:T(8,128)(2,1)}, u32[]{:S(2)}) copy-start(bf16[1,512,768]{2,1,0:T(8,128)(2,1)} %param.19) | copy-start | bytes 2359300
  91.0 21.4 %copy-start.30 = (bf16[4,128,768]{1,2,0:T(8,128)(2,1)}, bf16[4,128,768]{1,2,0:T(8,128)(2,1)S(1)}, u32[]{:S(2)}) copy-start(bf16[4,128,768]{1,2,0:T(8,128)(2,1)S(1)} %copy.119) | copy-start | bytes 2359300
  115.0 32.4 %copy-start.20 = (bf16[4,12,64,128]{3,2,1,0:T(8,128)(2,1)}, bf16[4,12,64,128]{3,2,1,0:T(8,128)(2,1)S(1)}, u32[]{:S(2)}) copy-start(bf16[4,12,64,128]{3,2,1,0:T(8,128)(2,1)S(1)} %convolution_convert_fusion.5) | copy-start | bytes 2359300
  147.1 193.7 %copy-start.75 = (f32[4,128]{1,0:T(4,128)}, f32[4,128]{1,0:T(4,128)S(1)}, u32[]{:S(2)}) copy-start(f32[4,128]{1,0:T(4,128)S(1)} %broadcast_multiply_fusion.11) | copy-start | bytes 6148
  147.4 95.4 %copy-start.77 = (f32[4,128]{1,0:T(4,128)}, f32[4,128]{1,0:T(4,128)S(1)}, u32[]{:S(2)}) copy-start(f32[4,128]{1,0:T(4,128)S(1)} %multiply_reduce_fusion.6) | copy-start | bytes 6148
  147.4 193.3 %copy-start.97 = (f32[4,128]{1,0:T(4,128)}, f32[4,128]{1,0:T(4,128)S(1)}, u32[]{:S(2)}) copy-start(f32[4,128]{1,0:T(4,128)S(1)} %fusion.95) | copy-start | bytes 6148
  365.9 7.8 copy-start.49
  378.3 11.4 copy-start.106
  381.7 7.9 copy-start.53
  381.7 10.3 slice-start
  381.7 10.3 slice-start.1
  394.8 9.6 copy-start.50
  395.4 9.9 copy-start.104
  408.3 8.1 copy-start.63
  408.3 8.1 copy-start.67
  408.3 8.1 copy-start.74
  418.7 10.1 slice-start.3
  419.5 9.3 copy-start.38
  420.1 8.7 slice-start.4
  420.1 8.7 slice-start.5
  420.1 8.7 copy-start.76
  420.1 8.7 copy-start.86
  420.1 8.7 copy-start.98
  450.7 78.0 %reduce-scatter.40.cloned.1.call-start = ((), (), s32[]{:S(2)}) async-start(), calls=%async_computation.22 | async-start | bytes 2949120
  458.8 110.4 %reduce-scatter.48.cloned.1.call-start = ((), (), s32[]{:S(2)}) async-start(), calls=%async_computation.26 | async-start | bytes 2949120
  469.3 140.3 %reduce-scatter.52.cloned.1.call-start = ((), (), s32[]{:S(2)}) async-start(), calls=%async_computation.28 | async-start | bytes 2949120
  472.9 177.1 %reduce-scatter.54.cloned.1.call-start = ((), (), s32[]{:S(2)}) async-start(), calls=%async_computation.29 | async-start | bytes 2949120
  475.8 214.6 %reduce-scatter.50.cloned.1.call-start = ((), (), s32[]{:S(2)}) async-start(), calls=%async_computation.27 | async-start | bytes 2949120
  477.9 253.5 %reduce-scatter.42.cloned.1.call-start = ((), (), s32[]{:S(2)}) async-start(), calls=%async_computation.23 | async-start | bytes 2949120
  479.8 291.9 %reduce-scatter.46.cloned.1.call-start = ((), (), s32[]{:S(2)}) async-start(), calls=%async_computation.25 | async-start | bytes 2949120
  481.8 387.9 %reduce-scatter.32.cloned.1.call-start = ((), (), s32[]{:S(2)}) async-start(), calls=%async_computation.18 | async-start | bytes 11796480 | tf_op jit(solution)/shard_map/reduce_scatter | solution.py:327
  489.1 478.5 %reduce-scatter.36.cloned.1.call-start = ((), (), s32[]{:S(2)}) async-start(), calls=%async_computation.20 | async-start | bytes 11796480 | tf_op jit(solution)/shard_map/reduce_scatter | solution.py:329
  497.2 568.3 %reduce-scatter.38.cloned.1.call-start = ((), (), s32[]{:S(2)}) async-start(), calls=%async_computation.21 | async-start | bytes 11796480 | tf_op jit(solution)/shard_map/reduce_scatter | solution.py:344
  504.2 659.1 %reduce-scatter.34.cloned.1.call-start = ((), (), s32[]{:S(2)}) async-start(), calls=%async_computation.19 | async-start | bytes 11796480 | tf_op jit(solution)/shard_map/reduce_scatter | solution.py:342
  510.3 7.1 copy-start.81
  510.3 8.3 copy-start.83
  510.3 8.9 copy-start.95
  510.3 707.3 %all-reduce.26.cloned.1.call-start = ((), (), s32[]{:S(2)}) async-start(), calls=%async_computation.32 | async-start | bytes 180224
  519.8 725.3 %reduce-scatter.56.cloned.1.call-start = ((), (), s32[]{:S(2)}) async-start(), calls=%async_computation.30 | async-start | bytes 491520
  520.8 1043.6 %all-reduce.24.cloned.1.call-start = ((), (), s32[]{:S(2)}) async-start(), calls=%async_computation.31 | async-start | bytes 31457280 | tf_op jit(solution)/shard_map/psum | solution.py:350
  (75 other events, 201.6 us)
Sparse Core Ops, SparseCore 0:
  9.8 55.4 all-gather.8
  67.1 38.4 all-gather.10
  107.5 37.3 all-gather.12
  146.5 96.1 all-gather.14
  244.5 96.1 all-gather.16
  450.8 37.3 reduce-scatter.43
  491.3 37.3 reduce-scatter.39
  531.7 37.3 reduce-scatter.47
  572.2 37.3 reduce-scatter.51
  612.5 37.3 reduce-scatter.53
  653.0 37.3 reduce-scatter.49
  693.9 37.3 reduce-scatter.41
  734.4 37.3 reduce-scatter.45
  774.7 94.8 reduce-scatter.31
  872.6 94.8 reduce-scatter.35
  970.5 94.8 reduce-scatter.37
  1068.4 94.8 reduce-scatter.33
  1169.2 48.4 all-reduce.25
  1220.4 24.6 reduce-scatter.55
  1249.6 314.8 all-reduce.23
